TPU v7x, 32 devices: a whole 2x2x4 slice. The times are simulated.
32 devices in a mesh: subj: 4 (over y, x), depth: 8 (over z, core).
Axes of the slice: x: 2, y: 2, z: 4, core: 2. Of those that a mesh axis runs over, the one named last changes fastest.
Arguments:
- images: float32 [4, 40, 128, 128], P('subj', 'depth'), may hold values from -6 to 6
- velocity: float32 [3, 4, 40, 128, 128], P(None, 'subj', 'depth'), may hold values from -3 to 3
- ref_index: int32 [4], replicated, may hold values from 0 to 3
- ref_weights: int32 [4, 4], P('subj'), may hold values from 0 to 16
Outputs:
- velocity_out: float32 [3, 4, 40, 128, 128], P(None, 'subj', 'depth')
Inputs may be any that keep to these rules, and one draw needn't show every extreme that they name: `ref_index`: subject indices of the references; they may repeat. `ref_weights`: numerators over 16.
All inputs are finite; a program needn't handle non-finite values.
Results may differ from a plain program's by a relative error of at most 0.0003.
Values sent between devices are 32-bit elements; how exact they have to be, the bound alone decides.
No kernel may reach another device: no remote copies, remote signals or barrier semaphores. Data moves between devices by JAX's collectives and lax.ppermute only.
A program may use at most 64 MiB of HBM per device.

v0:
```python
import math

import jax
import jax.numpy as jnp
from jax import lax
from jax.sharding import PartitionSpec as P

X = 128
Y = 128
ZD = 5
SUBJ_DEV = 1
NREF = 4
WIN = 9
RG = 3
WDEN = 16


def padded(shard, sides, width):
    for axis, dim in sides:
        devices, length = (lax.axis_size(axis), shard.shape[dim])
        up = [(i, (i + 1) % devices) for i in range(devices - 1)]
        down = [(j, i) for i, j in up]
        last = lax.slice_in_dim(shard, length - width, length, axis=dim)
        first = lax.slice_in_dim(shard, 0, width, axis=dim)
        before = lax.ppermute(last, axis, up)
        after = lax.ppermute(first, axis, down)
        shard = jnp.concatenate([before, shard, after], axis=dim)
    return shard


def gauss_taps():
    raw = [math.exp(-0.5 * offset * offset) for offset in range(-RG, RG + 1)]
    total = sum(raw)
    return [value / total for value in raw]


def band_matrix(length, taps):
    radius = len(taps) // 2
    rows_idx = lax.broadcasted_iota(jnp.int32, (length, length), 0)
    cols_idx = lax.broadcasted_iota(jnp.int32, (length, length), 1)
    matrix = jnp.zeros((length, length), jnp.float32)
    for offset in range(len(taps)):
        matrix = matrix + jnp.where(rows_idx - cols_idx == offset - radius, taps[offset], 0.0)
    return matrix


def planes_xy(field, matrix_x, matrix_y):
    across = jnp.dot(field, matrix_y, precision=lax.Precision.HIGHEST)
    return jnp.einsum("wx,pxy->pwy", matrix_x, across, precision=lax.Precision.HIGHEST)


def depth_window(field, taps, planes, axis):
    total = taps[0] * lax.slice_in_dim(field, 0, planes, axis=axis)
    for offset in range(1, len(taps)):
        total = total + taps[offset] * lax.slice_in_dim(field, offset, offset + planes, axis=axis)
    return total


def boxed(field, box_x, box_y):
    summed = depth_window(field, [1.0] * WIN, ZD, 0)
    return planes_xy(summed, box_x, box_y) / float(WIN**3)


def on_device(images, velocity, ref_index, ref_weights):
    radius = WIN // 2
    ones_taps = [1.0] * WIN
    box_x = band_matrix(X, ones_taps)
    box_y = band_matrix(Y, ones_taps)
    taps = gauss_taps()
    smooth_x = band_matrix(X, taps)
    smooth_y = band_matrix(Y, taps)
    own_ext = padded(images, (("depth", 1),), radius + 1)
    everyone = lax.all_gather(images, "subj", axis=0, tiled=True)
    picked = everyone[ref_index]
    ref_ext = padded(picked, (("depth", 1),), radius)
    moving_ext = own_ext[0]
    inner = moving_ext[1:-1]
    core = moving_ext[radius + 1 : radius + 1 + ZD]
    mean_i = boxed(inner, box_x, box_y)
    var_i = boxed(inner * inner, box_x, box_y) - mean_i * mean_i + 1e-05
    coeffs = jnp.zeros_like(core)
    for refnum in range(NREF):
        fixed_ext = ref_ext[refnum]
        fixed_core = fixed_ext[radius : radius + ZD]
        mean_j = boxed(fixed_ext, box_x, box_y)
        var_j = boxed(fixed_ext * fixed_ext, box_x, box_y) - mean_j * mean_j + 1e-05
        covariance = boxed(inner * fixed_ext, box_x, box_y) - mean_i * mean_j
        term = (
            2.0
            * covariance
            / (var_i * var_j)
            * (fixed_core - mean_j - covariance / var_i * (core - mean_i))
        )
        coeffs = coeffs + ref_weights[0, refnum].astype(jnp.float32) / float(WDEN) * term
    grad_depth = (moving_ext[radius + 2 : radius + 2 + ZD] - moving_ext[radius : radius + ZD]) * 0.5
    pad_x = jnp.pad(core, ((0, 0), (1, 1), (0, 0)))
    grad_x = (pad_x[:, 2:, :] - pad_x[:, :-2, :]) * 0.5
    pad_y = jnp.pad(core, ((0, 0), (0, 0), (1, 1)))
    grad_y = (pad_y[:, :, 2:] - pad_y[:, :, :-2]) * 0.5
    forces = [jnp.stack([coeffs * grad_depth, coeffs * grad_x, coeffs * grad_y])]
    force_all = jnp.stack(forces, axis=1)
    force_ext = padded(force_all, (("depth", 2),), RG)
    summed = depth_window(force_ext, taps, ZD, 2)
    flat = summed.reshape((3 * SUBJ_DEV * ZD, X, Y))
    smooth = planes_xy(flat, smooth_x, smooth_y).reshape((3, SUBJ_DEV, ZD, X, Y))
    return velocity + 40.0 * smooth


def solution(mesh):
    placed = (
        P("subj", "depth", None, None),
        P(None, "subj", "depth", None, None),
        P(),
        P("subj", None),
    )
    return jax.shard_map(
        on_device,
        mesh=mesh,
        in_specs=placed,
        out_specs=P(None, "subj", "depth", None, None),
        check_vma=False,
    )
```

profile of v0, /device:TPU:1, one launch (start us, length us, event | category | flops | bytes accessed | tf_op | source)
XLA Modules:
  0.0 104.2 jit_solution(750926797354328211)
XLA Ops:
  6.5 0.7 all-gather.2.cloned.1.call-update
  7.3 1.1 %copy.28 = f32[1,5,128,128]{2,3,1,0:T(8,128)S(1)} copy(f32[1,5,128,128]{3,2,1,0:T(8,128)} %param.4) | data formatting | bytes 655360 | tf_op args[0]
  8.4 1.9 %collective-permute-start.1 = (f32[1,5,128,128]{2,3,1,0:T(8,128)S(1)}, f32[1,5,128,128]{2,3,1,0:T(8,128)S(1)}, u32[]{:S(2)}, u32[]{:S(2)}) collective-permute-start(f32[1,5,128,128]{2,3,1,0:T(8,128)S(1)} %copy.28), channel_id=1, source_target_pairs={{1,0},{2,1},{3,2},{4,3},{5,4},{6,5},{7,6},{9,8},{10,9},{11,10},{12... | collective-permute-start | bytes 983048 | tf_op jit(solution)/shard_map/ppermute | solution.py:26
  10.3 4.6 %collective-permute-start = (f32[1,5,128,128]{2,3,1,0:T(8,128)S(1)}, f32[1,5,128,128]{2,3,1,0:T(8,128)}, u32[]{:S(2)}, u32[]{:S(2)}) collective-permute-start(f32[1,5,128,128]{2,3,1,0:T(8,128)S(1)} %copy.28), channel_id=1, source_target_pairs={{0,1},{1,2},{2,3},{3,4},{4,5},{5,6},{6,7},{8,9},{9,10},{10,11},{11... | collective-permute-start | bytes 983048 | tf_op jit(solution)/shard_map/ppermute | solution.py:25
  14.9 1.5 %fusion.643 = (s32[1,1]{1,0:T(1,128)}, s32[1,1]{1,0:T(1,128)}, s32[1,1]{1,0:T(1,128)}, s32[1,1]{1,0:T(1,128)}) fusion(s32[1,4]{1,0:T(1,128)} %param.7), kind=kLoop, calls=%fused_computation.796 | loop fusion | bytes 32 | tf_op jit(solution)/shard_map/slice | solution.py:94
  16.4 0.7 compare_select_fusion
  19.5 20.2 %all-gather.2.cloned.1.call-done = f32[4,5,128,128]{3,2,1,0:T(8,128)} async-done(((f32[1,5,128,128]{3,2,1,0:T(8,128)}), f32[4,5,128,128]{3,2,1,0:T(8,128)}) %all-gather.2.cloned.1.call-update) | async-done | bytes 1310736 | tf_op jit(solution)/shard_map/all_gather | solution.py:73
  39.8 1.9 %gather_fusion = f32[4,5,128,128]{3,2,1,0:T(8,128)S(1)} fusion(f32[4,5,128,128]{3,2,1,0:T(8,128)} %all-gather.2.cloned.1.call-done, s32[1024]{0:T(1024)S(1)} %pad_clamp_fusion), kind=kCustom, calls=%fused_computation | custom fusion | bytes 2621456 | tf_op jit(solution)/shard_map/gather | solution.py:74
  42.4 3.8 %collective-permute-start.2 = (f32[4,4,128,128]{2,3,1,0:T(8,128)S(1)}, f32[4,4,128,128]{2,3,1,0:T(8,128)S(1)}, u32[]{:S(2)}, u32[]{:S(2)}) collective-permute-start(f32[4,4,128,128]{2,3,1,0:T(8,128)S(1)} %get-tuple-element.12), channel_id=1, source_target_pairs={{0,1},{1,2},{2,3},{3,4},{4,5},{5,6},{6,7},{8,9},{9,10},{10,11},{11... | collective-permute-start | bytes 3145736 | tf_op jit(solution)/shard_map/ppermute | solution.py:25
  46.2 1.9 %collective-permute-start.3 = (f32[4,4,128,128]{2,3,1,0:T(8,128)S(1)}, f32[4,4,128,128]{2,3,1,0:T(8,128)S(1)}, u32[]{:S(2)}, u32[]{:S(2)}) collective-permute-start(f32[4,4,128,128]{2,3,1,0:T(8,128)S(1)} %get-tuple-element.13), channel_id=1, source_target_pairs={{1,0},{2,1},{3,2},{4,3},{5,4},{6,5},{7,6},{9,8},{10,9},{11,10},{12... | collective-permute-start | bytes 3145736 | tf_op jit(solution)/shard_map/ppermute | solution.py:26
  48.2 1.0 fusion.640
  49.8 1.6 %fusion.73 = f32[5,128,128]{1,2,0:T(8,128)S(1)} fusion(f32[1,5,128,128]{2,3,1,0:T(8,128)S(1)} %copy.28, f32[1,5,128,128]{2,3,1,0:T(8,128)S(1)} %collective-permute-done.1, f32[1,5,128,128]{2,3,1,0:T(8,128)} %collective-permute-done), kind=kOutput, calls=%fused_computation.188 | convolution fusion | flops 127582208 | bytes 1310720 | tf_op jit(solution)/shard_map/dot_general | solution.py:48
  52.4 5.6 %collective-permute-done.2 = f32[4,4,128,128]{2,3,1,0:T(8,128)S(1)} collective-permute-done((f32[4,4,128,128]{2,3,1,0:T(8,128)S(1)}, f32[4,4,128,128]{2,3,1,0:T(8,128)S(1)}, u32[]{:S(2)}, u32[]{:S(2)}) %collective-permute-start.2) | collective-permute-done | bytes 1048608 | tf_op jit(solution)/shard_map/ppermute | solution.py:25
  57.9 4.4 %collective-permute-done.3 = f32[4,4,128,128]{2,3,1,0:T(8,128)S(1)} collective-permute-done((f32[4,4,128,128]{2,3,1,0:T(8,128)S(1)}, f32[4,4,128,128]{2,3,1,0:T(8,128)S(1)}, u32[]{:S(2)}, u32[]{:S(2)}) %collective-permute-start.3) | collective-permute-done | bytes 1048608 | tf_op jit(solution)/shard_map/ppermute | solution.py:26
  62.3 0.6 fusion.122
  63.4 0.6 fusion.105
  64.5 0.6 fusion.139
  65.5 0.6 fusion.97
  67.5 1.9 %slice_multiply_fusion.7 = (f32[1,13,128,128]{2,3,1,0:T(8,128)S(1)}, f32[1,13,128,128]{2,3,1,0:T(8,128)S(1)}, f32[1,13,128,128]{2,3,1,0:T(8,128)S(1)}, f32[1,13,...) fusion(f32[4,13,128,128]{2,3,1,0:T(8,128)S(1)} %pad_maximum_fus, ...), kind=kLoop, calls=%fused_computation.173 | loop fusion | flops 1916928 | bytes 10354688 | tf_op jit(solution)/shard_map/mul | solution.py:87
  69.4 0.6 fusion.253
  74.0 0.7 fusion.4
  75.6 0.6 fusion.46
  76.2 0.6 fusion.36
  76.8 0.6 fusion.41
  77.4 1.6 %fusion.638 = (f32[1,1,5,128,128]{3,4,2,1,0:T(8,128)S(1)}, f32[1,1,5,128,128]{3,4,2,1,0:T(8,128)S(1)}, f32[1,5,128,128]{2,3,1,0:T(8,128)S(1)}, f32[1,5,128,128]{2,3,1,0:T(8,128)S(1)}, f32[5,128,128]{1,2,0:T(8,128)S(1)}) fusion(f32[5,128,128]{1,2,0:T(8,128)S(1)} %bitcast.441, f32[1,5,128,128]{2,3,1,0:T(8,128)S(1)} %copy.28, ...), kind=kOutput, calls=%fused_computation.791 | convolution fusion | flops 128974848 | bytes 5898244 | tf_op jit(solution)/shard_map/wx,pxy->pwy/dot_general | solution.py:49
  79.2 1.9 %collective-permute-start.4 = (f32[3,1,3,128,128]{3,4,2,1,0:T(8,128)S(1)}, f32[3,1,3,128,128]{3,4,2,1,0:T(8,128)S(1)}, u32[]{:S(2)}, u32[]{:S(2)}) collective-permute-start(f32[3,1,3,128,128]{3,4,2,1,0:T(8,128)S(1)} %get-tuple-element.14), channel_id=1, source_target_pairs={{0,1},{1,2},{2,3},{3,4},{4,5},{5,6},{6,7},{8,9},{9,10},{10,11},{11... | collective-permute-start | bytes 1769480 | tf_op jit(solution)/shard_map/ppermute | solution.py:25
  81.2 2.4 %collective-permute-start.5 = (f32[3,1,3,128,128]{3,4,2,1,0:T(8,128)S(1)}, f32[3,1,3,128,128]{3,4,2,1,0:T(8,128)S(1)}, u32[]{:S(2)}, u32[]{:S(2)}) collective-permute-start(f32[3,1,3,128,128]{3,4,2,1,0:T(8,128)S(1)} %get-tuple-element.15), channel_id=1, source_target_pairs={{1,0},{2,1},{3,2},{4,3},{5,4},{6,5},{7,6},{9,8},{10,9},{11,10},{12... | collective-permute-start | bytes 1769480 | tf_op jit(solution)/shard_map/ppermute | solution.py:26
  83.6 4.4 %collective-permute-done.4 = f32[3,1,3,128,128]{3,4,2,1,0:T(8,128)S(1)} collective-permute-done((f32[3,1,3,128,128]{3,4,2,1,0:T(8,128)S(1)}, f32[3,1,3,128,128]{3,4,2,1,0:T(8,128)S(1)}, u32[]{:S(2)}, u32[]{:S(2)}) %collective-permute-start.4) | collective-permute-done | bytes 589856 | tf_op jit(solution)/shard_map/ppermute | solution.py:25
  88.0 4.4 %collective-permute-done.5 = f32[3,1,3,128,128]{3,4,2,1,0:T(8,128)S(1)} collective-permute-done((f32[3,1,3,128,128]{3,4,2,1,0:T(8,128)S(1)}, f32[3,1,3,128,128]{3,4,2,1,0:T(8,128)S(1)}, u32[]{:S(2)}, u32[]{:S(2)}) %collective-permute-start.5) | collective-permute-done | bytes 589856 | tf_op jit(solution)/shard_map/ppermute | solution.py:26
  92.8 1.0 fusion.258
  93.8 1.0 convolution_multiply_fusion
  95.1 2.3 %add.1112 = f32[3,1,5,128,128]{4,3,2,1,0:T(8,128)} add(f32[3,1,5,128,128]{4,3,2,1,0:T(8,128)} %param.5, f32[3,1,5,128,128]{4,3,2,1,0:T(8,128)S(1)} %copy.73) | non-fusion elementwise | flops 245760 | bytes 2949120 | tf_op jit(solution)/shard_map/add | solution.py:106
  (29 shorter events, 10.7 us)
Async XLA Ops:
  6.5 33.2 %all-gather.2.cloned.1.call-start = ((), (), s32[]{:S(2)}) async-start(), calls=%async_computation | async-start | bytes 1638400 | tf_op jit(solution)/shard_map/all_gather | solution.py:73
  8.4 39.8 %collective-permute-start.1 = (f32[1,5,128,128]{2,3,1,0:T(8,128)S(1)}, f32[1,5,128,128]{2,3,1,0:T(8,128)S(1)}, u32[]{:S(2)}, u32[]{:S(2)}) collective-permute-start(f32[1,5,128,128]{2,3,1,0:T(8,128)S(1)} %copy.28), channel_id=1, source_target_pairs={{1,0},{2,1},{3,2},{4,3},{5,4},{6,5},{7,6},{9,8},{10,9},{11,10},{12... | collective-permute-start | bytes 983048 | tf_op jit(solution)/shard_map/ppermute | solution.py:26
  10.3 37.8 %collective-permute-start = (f32[1,5,128,128]{2,3,1,0:T(8,128)S(1)}, f32[1,5,128,128]{2,3,1,0:T(8,128)}, u32[]{:S(2)}, u32[]{:S(2)}) collective-permute-start(f32[1,5,128,128]{2,3,1,0:T(8,128)S(1)} %copy.28), channel_id=1, source_target_pairs={{0,1},{1,2},{2,3},{3,4},{4,5},{5,6},{6,7},{8,9},{9,10},{10,11},{11... | collective-permute-start | bytes 983048 | tf_op jit(solution)/shard_map/ppermute | solution.py:25
  42.4 15.6 %collective-permute-start.2 = (f32[4,4,128,128]{2,3,1,0:T(8,128)S(1)}, f32[4,4,128,128]{2,3,1,0:T(8,128)S(1)}, u32[]{:S(2)}, u32[]{:S(2)}) collective-permute-start(f32[4,4,128,128]{2,3,1,0:T(8,128)S(1)} %get-tuple-element.12), channel_id=1, source_target_pairs={{0,1},{1,2},{2,3},{3,4},{4,5},{5,6},{6,7},{8,9},{9,10},{10,11},{11... | collective-permute-start | bytes 3145736 | tf_op jit(solution)/shard_map/ppermute | solution.py:25
  46.2 16.1 %collective-permute-start.3 = (f32[4,4,128,128]{2,3,1,0:T(8,128)S(1)}, f32[4,4,128,128]{2,3,1,0:T(8,128)S(1)}, u32[]{:S(2)}, u32[]{:S(2)}) collective-permute-start(f32[4,4,128,128]{2,3,1,0:T(8,128)S(1)} %get-tuple-element.13), channel_id=1, source_target_pairs={{1,0},{2,1},{3,2},{4,3},{5,4},{6,5},{7,6},{9,8},{10,9},{11,10},{12... | collective-permute-start | bytes 3145736 | tf_op jit(solution)/shard_map/ppermute | solution.py:26
  79.2 8.7 %collective-permute-start.4 = (f32[3,1,3,128,128]{3,4,2,1,0:T(8,128)S(1)}, f32[3,1,3,128,128]{3,4,2,1,0:T(8,128)S(1)}, u32[]{:S(2)}, u32[]{:S(2)}) collective-permute-start(f32[3,1,3,128,128]{3,4,2,1,0:T(8,128)S(1)} %get-tuple-element.14), channel_id=1, source_target_pairs={{0,1},{1,2},{2,3},{3,4},{4,5},{5,6},{6,7},{8,9},{9,10},{10,11},{11... | collective-permute-start | bytes 1769480 | tf_op jit(solution)/shard_map/ppermute | solution.py:25
  81.2 11.2 %collective-permute-start.5 = (f32[3,1,3,128,128]{3,4,2,1,0:T(8,128)S(1)}, f32[3,1,3,128,128]{3,4,2,1,0:T(8,128)S(1)}, u32[]{:S(2)}, u32[]{:S(2)}) collective-permute-start(f32[3,1,3,128,128]{3,4,2,1,0:T(8,128)S(1)} %get-tuple-element.15), channel_id=1, source_target_pairs={{1,0},{2,1},{3,2},{4,3},{5,4},{6,5},{7,6},{9,8},{10,9},{11,10},{12... | collective-permute-start | bytes 1769480 | tf_op jit(solution)/shard_map/ppermute | solution.py:26
Sparse Core Ops, SparseCore 0:
  9.2 30.5 all-gather.1
where the time goes:
time: 105 us; the launch traced here: 104 us
  waiting for transfers between devices  39.7 us (38%)
  matrix products  19.4 us (18%)
  starting transfers between devices  16.6 us (16%)
  between operations  16.3 us (16%)
  other arithmetic  6.7 us (6%)
  local copies, waits for them, and re-layouts  5.59 us (5%)
    all_gather x1, waiting for transfers between devices, on_device(): everyone = lax.all_gather(images, 'subj', axis=0, tiled=True)  20.2 us
    ppermute x3, starting transfers between devices, padded(): before = lax.ppermute(last, axis, up)  10.3 us
    dot_general x15, matrix products, planes_xy(): across = jnp.dot(field, matrix_y, precision=lax.Precision.HIGHEST)  10.2 us
    ppermute x3, waiting for transfers between devices, padded(): before = lax.ppermute(last, axis, up)  9.91 us
    dot_general x15, matrix products, planes_xy(): jnp.einsum('wx,pxy->pwy', matrix_x, across, precision=lax.Precision.HIGHEST)  9.25 us
    ppermute x3, waiting for transfers between devices, padded(): after = lax.ppermute(first, axis, down)  8.79 us
    ppermute x3, starting transfers between devices, padded(): after = lax.ppermute(first, axis, down)  6.29 us
    gather x2, local copies, waits for them, and re-layouts, on_device(): picked = everyone[ref_index]  2.34 us
  transfers between devices with their start and end apart: 7, of which 5 were waited for; matrix products, arithmetic and copies ran while one was open for 10% of the time, Pallas kernels for 0%

commit v1 on v0

v1 whole, which is shorter than its diff:
```python
import functools
import math

import jax
import jax.numpy as jnp
from jax import lax
from jax.experimental import pallas as pl
from jax.experimental.pallas import tpu as pltpu
from jax.sharding import PartitionSpec as P

WIN = 9
RAD = WIN // 2
RG = 3
WDEN = 16
STRIP = 16
PAD = 8


def gauss_taps():
    raw = [math.exp(-0.5 * offset * offset) for offset in range(-RG, RG + 1)]
    total = sum(raw)
    return [value / total for value in raw]


def band(size, taps, dtype):
    radius = len(taps) // 2
    rows = lax.broadcasted_iota(jnp.int32, (size, size), 0)
    cols = lax.broadcasted_iota(jnp.int32, (size, size), 1)
    gap = rows - cols
    matrix = jnp.zeros((size, size), jnp.float32)
    for offset, tap in enumerate(taps):
        matrix = jnp.where(gap == offset - radius, tap, matrix)
    return matrix.astype(dtype) if dtype is not None else matrix


def split3(value):
    hi = value.astype(jnp.bfloat16)
    rest = value - hi.astype(jnp.float32)
    mid = rest.astype(jnp.bfloat16)
    lo = (rest - mid.astype(jnp.float32)).astype(jnp.bfloat16)
    return hi, mid, lo


def depth_planes(refs, low_core, rows, reach):
    core, near, far = refs
    depth = core.shape[0]
    start = near.shape[0] - reach
    planes = [
        jnp.where(low_core, far[start + i, rows, :], near[start + i, rows, :])
        for i in range(reach)
    ]
    planes += [core[p, rows, :] for p in range(depth)]
    planes += [
        jnp.where(low_core, near[i, rows, :], far[i, rows, :]) for i in range(reach)
    ]
    return planes


def window_sums(planes, depth):
    reach = (len(planes) - depth) // 2
    if depth > 2 * reach + 1:
        return [sum(planes[p + 1 : p + 2 * reach + 1], planes[p]) for p in range(depth)]
    first, last = depth - 1, 2 * reach
    common = planes[first]
    for p in range(first + 1, last + 1):
        common = common + planes[p]
    left = [None] * depth
    run = None
    for p in range(first - 1, -1, -1):
        run = planes[p] if run is None else run + planes[p]
        left[p] = run
    right = [None] * depth
    run = None
    for p in range(last + 1, last + depth):
        run = planes[p] if run is None else run + planes[p]
        right[p - last] = run
    sums = []
    for p in range(depth):
        total = common
        if left[p] is not None:
            total = total + left[p]
        if right[p] is not None:
            total = total + right[p]
        sums.append(total)
    return sums


def clear_pads(sums_ref, width):
    count, _, lanes = sums_ref.shape
    zeros = jnp.zeros((count, PAD, lanes), jnp.float32)
    sums_ref[:, 0:PAD, :] = zeros
    sums_ref[:, PAD + width : 2 * PAD + width, :] = zeros


def box_strip(sums_ref, count, start, matrix):
    parts = []
    for f in range(count):
        total = sums_ref[f, pl.ds(start + PAD - RAD, STRIP), :]
        for k in range(1, WIN):
            total = total + sums_ref[f, pl.ds(start + PAD - RAD + k, STRIP), :]
        parts.append(total)
    stacked = jnp.concatenate(parts, axis=0)
    wide = jnp.concatenate(split3(stacked), axis=1)
    out = jnp.dot(wide, matrix, preferred_element_type=jnp.float32)
    out = out * (1.0 / float(WIN**3))
    return [out[f * STRIP : (f + 1) * STRIP, :] for f in range(count)]


def weight_of(index_ref, weights_ref, subject):
    total = jnp.int32(0)
    for r in range(index_ref.shape[0]):
        total = total + jnp.where(index_ref[r] == subject, weights_ref[0, r], 0)
    return total.astype(jnp.float32) / float(WDEN)


def box_matrix(size):
    one = band(size, [1.0] * WIN, jnp.bfloat16)
    return jnp.concatenate([one, one, one], axis=0)


def own_kernel(pick, core, near, far, *rest):
    index_ref, weights_ref, window_ref, mean_ref, inv_ref, acc_ref, grads_ref, sums_ref, wide_ref = rest
    depth, width, lanes = core.shape
    reach = depth + 2 * RG
    low_core = lax.axis_index("depth") % 2 == 0
    clear_pads(sums_ref, width)
    clear_pads(wide_ref, width)

    def gather(i, carry):
        start = pl.multiple_of(i * STRIP, STRIP)
        rows = pl.ds(start, STRIP)
        planes = depth_planes((core, near, far), low_core, rows, RAD)
        for p, value in enumerate(planes):
            window_ref[p, rows, :] = value
            wide_ref[p, pl.ds(start + PAD, STRIP), :] = value
        for f, field in enumerate((planes, [v * v for v in planes])):
            for p, total in enumerate(window_sums(field, depth)):
                sums_ref[f * depth + p, pl.ds(start + PAD, STRIP), :] = total
        return carry

    lax.fori_loop(0, width // STRIP, gather, 0)
    matrix = box_matrix(lanes)
    weight = jnp.float32(0.0)
    if pick is not None:
        weight = weight_of(index_ref, weights_ref, lax.axis_index("subj"))
    column = lax.broadcasted_iota(jnp.int32, (STRIP, lanes), 1)

    def finish(i, carry):
        start = pl.multiple_of(i * STRIP, STRIP)
        rows = pl.ds(start, STRIP)
        boxes = box_strip(sums_ref, 2 * depth, start, matrix)
        for p in range(depth):
            mean = boxes[p]
            cov = boxes[depth + p] - mean * mean
            inv = 1.0 / (cov + 1e-05)
            gap = core[p, rows, :] - mean
            ratio = cov * inv
            mean_ref[p, rows, :] = mean
            inv_ref[p, rows, :] = inv
            acc_ref[p, rows, :] = (weight * 2.0) * (ratio * inv) * (gap - ratio * gap)
        for p in range(reach):
            q = p + RAD - RG
            here = wide_ref[q, pl.ds(start + PAD, STRIP), :]
            above = wide_ref[q, pl.ds(start + PAD + 1, STRIP), :]
            below = wide_ref[q, pl.ds(start + PAD - 1, STRIP), :]
            front = wide_ref[q + 1, pl.ds(start + PAD, STRIP), :]
            back = wide_ref[q - 1, pl.ds(start + PAD, STRIP), :]
            right = jnp.where(column == lanes - 1, 0.0, pltpu.roll(here, lanes - 1, 1))
            left = jnp.where(column == 0, 0.0, pltpu.roll(here, 1, 1))
            grads_ref[p, rows, :] = (front - back) * 0.5
            grads_ref[reach + p, rows, :] = (above - below) * 0.5
            grads_ref[2 * reach + p, rows, :] = (right - left) * 0.5
        return carry

    lax.fori_loop(0, width // STRIP, finish, 0)


def pair_kernel(pick, last, jcore, jnear, jfar, window, mean_ref, inv_ref, acc_ref, index_ref, weights_ref, *rest):
    outs, sums_ref = rest[:-1], rest[-1]
    depth, width, lanes = jcore.shape
    low_core = lax.axis_index("depth") % 2 == 0
    if pick[0] == "xor":
        weight = weight_of(index_ref, weights_ref, lax.axis_index("subj") ^ pick[1])
    else:
        weight = weights_ref[0, pick[1]].astype(jnp.float32) / float(WDEN)
    clear_pads(sums_ref, width)

    def gather(i, carry):
        start = pl.multiple_of(i * STRIP, STRIP)
        rows = pl.ds(start, STRIP)
        mine = [window[p, rows, :] for p in range(depth + 2 * RAD)]
        planes = depth_planes((jcore, jnear, jfar), low_core, rows, RAD)
        fields = (planes, [v * v for v in planes], [a * b for a, b in zip(mine, planes)])
        for f, field in enumerate(fields):
            for p, total in enumerate(window_sums(field, depth)):
                sums_ref[f * depth + p, pl.ds(start + PAD, STRIP), :] = total
        return carry

    lax.fori_loop(0, width // STRIP, gather, 0)
    matrix = box_matrix(lanes)

    def finish(i, carry):
        start = pl.multiple_of(i * STRIP, STRIP)
        rows = pl.ds(start, STRIP)
        boxes = box_strip(sums_ref, 3 * depth, start, matrix)
        results = []
        for p in range(depth):
            mean_j = boxes[p]
            var_j = boxes[depth + p] - mean_j * mean_j + 1e-05
            mean_i = mean_ref[p, rows, :]
            inv_i = inv_ref[p, rows, :]
            cov = boxes[2 * depth + p] - mean_i * mean_j
            ratio = cov * inv_i
            gap = jcore[p, rows, :] - mean_j - ratio * (window[p + RAD, rows, :] - mean_i)
            term = (weight * 2.0) * ratio / var_j * gap
            results.append(acc_ref[p, rows, :] + term)
        for p in range(depth):
            outs[0][p, rows, :] = results[p]
        if last:
            for i in range(RG):
                low, high = results[i], results[depth - RG + i]
                outs[1][i, rows, :] = jnp.where(low_core, high, low)
                outs[2][i, rows, :] = jnp.where(low_core, low, high)
        return carry

    lax.fori_loop(0, width // STRIP, finish, 0)


def final_kernel(coeff, cnear, cfar, grads, velocity, out, force_ref, vel_ref, res_ref, in_sem, out_sem):
    depth, width, lanes = coeff.shape
    reach = depth + 2 * RG
    comps = 3
    load = pltpu.make_async_copy(velocity, vel_ref, in_sem)
    load.start()
    low_core = lax.axis_index("depth") % 2 == 0
    taps = gauss_taps()
    clear_pads(force_ref, width)

    def gather(i, carry):
        start = pl.multiple_of(i * STRIP, STRIP)
        rows = pl.ds(start, STRIP)
        weights = depth_planes((coeff, cnear, cfar), low_core, rows, RG)
        for f in range(comps):
            planes = [weights[p] * grads[f * reach + p, rows, :] for p in range(reach)]
            for p in range(depth):
                total = taps[RG] * planes[p + RG]
                for k in range(RG):
                    total = total + taps[k] * (planes[p + k] + planes[p + 2 * RG - k])
                force_ref[f * depth + p, pl.ds(start + PAD, STRIP), :] = total
        return carry

    lax.fori_loop(0, width // STRIP, gather, 0)
    full = band(lanes, taps, None)
    hi = full.astype(jnp.bfloat16)
    lo = (full - hi.astype(jnp.float32)).astype(jnp.bfloat16)
    matrix = jnp.concatenate([hi, hi, lo], axis=0)
    load.wait()

    def store(start, i):
        rows = pl.ds(start, STRIP)
        return pltpu.make_async_copy(res_ref.at[:, :, rows, :], out.at[:, 0, :, rows, :], out_sem.at[i])

    def finish(i, carry):
        start = pl.multiple_of(i * STRIP, STRIP)
        rows = pl.ds(start, STRIP)
        parts = []
        for f in range(comps * depth):
            rowed = [force_ref[f, pl.ds(start + PAD - RG + k, STRIP), :] for k in range(2 * RG + 1)]
            total = taps[RG] * rowed[RG]
            for k in range(RG):
                total = total + taps[k] * (rowed[k] + rowed[2 * RG - k])
            parts.append(total)
        stacked = jnp.concatenate(parts, axis=0)
        high = stacked.astype(jnp.bfloat16)
        low = (stacked - high.astype(jnp.float32)).astype(jnp.bfloat16)
        wide = jnp.concatenate([high, low, high], axis=1)
        smooth = jnp.dot(wide, matrix, preferred_element_type=jnp.float32)
        for f in range(comps):
            for p in range(depth):
                n = f * depth + p
                value = smooth[n * STRIP : (n + 1) * STRIP, :]
                res_ref[f, p, rows, :] = vel_ref[f, 0, p, rows, :] + 40.0 * value
        store(start, i).start()
        return carry

    lax.fori_loop(0, width // STRIP, finish, 0)
    for i in range(width // STRIP):
        store(i * STRIP, i).wait()


def f32(*shape):
    return jax.ShapeDtypeStruct(shape, jnp.float32)


def call(kernel, name, outs, scratch, n_vmem, n_smem, args, flops):
    whole = pl.BlockSpec(memory_space=pltpu.VMEM)
    small = pl.BlockSpec(memory_space=pltpu.SMEM)
    moved = sum(math.prod(a.shape) for a in args) + sum(math.prod(o.shape) for o in outs)
    return pl.pallas_call(
        kernel,
        name=name,
        out_shape=outs,
        in_specs=[whole] * n_vmem + [small] * n_smem,
        out_specs=[whole] * len(outs),
        scratch_shapes=scratch,
        cost_estimate=pl.CostEstimate(flops=flops, bytes_accessed=4 * moved, transcendentals=0),
    )(*args)


def on_device(images, velocity, ref_index, ref_weights):
    subjects = lax.axis_size("subj")
    stack = lax.axis_size("depth")
    own = images[0]
    depth, width, lanes = own.shape
    mate = [(i, i ^ 1) for i in range(stack)]
    hop = [(i, i + 2) for i in range(0, stack - 2, 2)] + [(i, i - 2) for i in range(3, stack, 2)]
    facing = [(i, i + 1) for i in range(1, stack - 1, 2)]
    facing = facing + [(j, i) for i, j in facing]

    def halos(slab):
        near = lax.ppermute(slab, "depth", mate)
        return near, lax.ppermute(near, "depth", hop)

    slabs = []
    if subjects <= ref_index.shape[0]:
        for k in range(1, subjects):
            swap = [(i, i ^ k) for i in range(subjects)]
            slabs.append((lax.ppermute(own, "subj", swap), ("xor", k)))
        self_pick = ("xor", 0)
    else:
        everyone = lax.all_gather(images, "subj", axis=0, tiled=True)
        for r in range(ref_index.shape[0]):
            slabs.append((everyone[ref_index[r]], ("ref", r)))
        self_pick = None

    near, far = halos(own)
    reach = depth + 2 * RG
    tall = width + 2 * PAD
    window, mean, inv, acc, grads = call(
        functools.partial(own_kernel, self_pick),
        "own",
        [f32(depth + 2 * RAD, width, lanes)] + [f32(depth, width, lanes)] * 3 + [f32(3 * reach, width, lanes)],
        [pltpu.VMEM((2 * depth, tall, lanes), jnp.float32), pltpu.VMEM((depth + 2 * RAD, tall, lanes), jnp.float32)],
        3,
        2,
        (own, near, far, ref_index, ref_weights),
        20_000_000,
    )
    for n, (slab, pick) in enumerate(slabs):
        last = n == len(slabs) - 1
        jnear, jfar = halos(slab)
        outs = [f32(depth, width, lanes)] + ([f32(RG, width, lanes)] * 2 if last else [])
        results = call(
            functools.partial(pair_kernel, pick, last),
            "pair",
            outs,
            [pltpu.VMEM((3 * depth, tall, lanes), jnp.float32)],
            7,
            2,
            (slab, jnear, jfar, window, mean, inv, acc, ref_index, ref_weights),
            20_000_000,
        )
        acc = results[0]
    cnear = lax.ppermute(results[1], "depth", mate)
    cfar = lax.ppermute(results[2], "depth", facing)
    whole = pl.BlockSpec(memory_space=pltpu.VMEM)
    away = pl.BlockSpec(memory_space=pl.ANY)
    return pl.pallas_call(
        final_kernel,
        name="smooth",
        out_shape=f32(3, 1, depth, width, lanes),
        in_specs=[whole] * 4 + [away],
        out_specs=away,
        scratch_shapes=[
            pltpu.VMEM((3 * depth, tall, lanes), jnp.float32),
            pltpu.VMEM((3, 1, depth, width, lanes), jnp.float32),
            pltpu.VMEM((3, depth, width, lanes), jnp.float32),
            pltpu.SemaphoreType.DMA,
            pltpu.SemaphoreType.DMA((width // STRIP,)),
        ],
        cost_estimate=pl.CostEstimate(flops=20_000_000, bytes_accessed=6_000_000, transcendentals=0),
    )(acc, cnear, cfar, grads, velocity)


def solution(mesh):
    placed = (
        P("subj", "depth", None, None),
        P(None, "subj", "depth", None, None),
        P(),
        P("subj", None),
    )
    return jax.shard_map(
        on_device,
        mesh=mesh,
        in_specs=placed,
        out_specs=P(None, "subj", "depth", None, None),
        check_vma=False,
    )
```

time: 105 us -> 67.4 us (0.64)
  waiting for transfers between devices: 39.7 us -> 13 us
  Pallas kernels: 0 us -> 24.4 us
  matrix products: 19.4 us -> 0 us
  between operations: 16.3 us -> 0.17 us
  starting transfers between devices: 16.6 us -> 26.5 us
  other arithmetic: 6.7 us -> 0 us
  local copies, waits for them, and re-layouts: 5.59 us -> 2.91 us
    pallas_call x0 -> x5, Pallas kernels: none -> 24.4 us  [the longest x4 18.8 us: call(): pl.pallas_call(kernel, name=name, out_shape=outs, in_specs=[whole] * n_vm...]
    all_gather x1 -> x0, waiting for transfers between devices: 20.2 us -> none  [on_device(): everyone = lax.all_gather(images, 'subj', axis=0, tiled=True)]
    dot_general x30 -> x0, matrix products: 19.4 us -> none  [the longest x15 10.2 us: planes_xy(): across = jnp.dot(field, matrix_y, precision=lax.Precision.HIGHEST)]
    ppermute x6 -> x13, starting transfers between devices: 16.6 us -> 26.5 us  [the longest x4 11 us: halos(): near = lax.ppermute(slab, 'depth', mate)]
    ppermute x6 -> x13, waiting for transfers between devices: 18.7 us -> 13 us  [the longest x1 5.25 us: on_device(): cfar = lax.ppermute(results[2], 'depth', facing)]
    mul x3 -> x0, other arithmetic: 2.99 us -> none  [the longest x1 1.9 us: on_device(): covariance = boxed(inner * fixed_ext, box_x, box_y) - mean_i * mean_j]
    add x2 -> x0, other arithmetic: 2.68 us -> none  [the longest x1 2.26 us: on_device(): return velocity + 40.0 * smooth]
    gather x2 -> x0, local copies, waits for them, and re-layouts: 2.34 us -> none  [on_device(): picked = everyone[ref_index]]
  transfers between devices with their start and end apart: 7 -> 13, of which waited for: 5 -> 3; matrix products, arithmetic and copies ran while one was open for 10% -> 0% of each run, Pallas kernels for 0% -> 21%
where the time goes in v1:
time: 67.4 us; the launch traced here: 67 us
  starting transfers between devices  26.5 us (39%)
  Pallas kernels  24.4 us (36%)
  waiting for transfers between devices  13 us (19%)
  local copies, waits for them, and re-layouts  2.91 us (4%)
    pallas_call x4, Pallas kernels, call(): pl.pallas_call(kernel, name=name, out_shape=outs, in_specs=[whole] * n_vm...  18.8 us
    ppermute x4, starting transfers between devices, halos(): near = lax.ppermute(slab, 'depth', mate)  11 us
    pallas_call x1, Pallas kernels, on_device(): pl.pallas_call(final_kernel, name='smooth', out_shape=f32(3, 1, depth, wi...  5.56 us
    ppermute x1, waiting for transfers between devices, on_device(): cfar = lax.ppermute(results[2], 'depth', facing)  5.25 us
    ppermute x4, starting transfers between devices, halos(): return (near, lax.ppermute(near, 'depth', hop))  5.16 us
    ppermute x3, waiting for transfers between devices, on_device(): slabs.append((lax.ppermute(own, 'subj', swap), ('xor', k)))  5.15 us
    ppermute x1, starting transfers between devices, on_device(): cnear = lax.ppermute(results[1], 'depth', mate)  5.12 us
    ppermute x3, starting transfers between devices, on_device(): slabs.append((lax.ppermute(own, 'subj', swap), ('xor', k)))  3.27 us
  transfers between devices with their start and end apart: 13, of which 3 were waited for; matrix products, arithmetic and copies ran while one was open for 0% of the time, Pallas kernels for 21%

profile of v1, /device:TPU:1, one launch (start us, length us, event | category | flops | bytes accessed | tf_op | source)
XLA Modules:
  0.0 67.0 jit_solution(2134886454881486887)
XLA Ops:
  0.0 2.0 %collective-permute-start.8 = (f32[5,128,128]{2,1,0:T(8,128)}, f32[5,128,128]{2,1,0:T(8,128)S(1)}, u32[]{:S(2)}, u32[]{:S(2)}) collective-permute-start(f32[5,128,128]{2,1,0:T(8,128)} %bitcast.1), channel_id=1, source_target_pairs={{0,8},{8,0},{16,24},{24,16},{1,9},{9,1},{17,25},{25,17},{2,10},{10... | collective-permute-start | bytes 983048 | tf_op jit(solution)/shard_map/ppermute | solution.py:328
  2.0 1.2 %collective-permute-start.5 = (f32[5,128,128]{2,1,0:T(8,128)}, f32[5,128,128]{2,1,0:T(8,128)S(1)}, u32[]{:S(2)}, u32[]{:S(2)}) collective-permute-start(f32[5,128,128]{2,1,0:T(8,128)} %bitcast.2), channel_id=1, source_target_pairs={{0,16},{8,24},{16,0},{24,8},{1,17},{9,25},{17,1},{25,9},{2,18},{10... | collective-permute-start | bytes 983048 | tf_op jit(solution)/shard_map/ppermute | solution.py:328
  3.3 0.0 collective-permute-start
  3.3 1.2 %collective-permute-start.3 = (f32[5,128,128]{2,1,0:T(8,128)}, f32[5,128,128]{2,1,0:T(8,128)S(1)}, u32[]{:S(2)}, u32[]{:S(2)}) collective-permute-start(f32[5,128,128]{2,1,0:T(8,128)} %bitcast.4), channel_id=1, source_target_pairs={{0,1},{1,0},{2,3},{3,2},{4,5},{5,4},{6,7},{7,6},{8,9},{9,8},{10,11... | collective-permute-start | bytes 983048 | tf_op jit(solution)/shard_map/ppermute | solution.py:321
  4.5 5.1 %collective-permute-done.8.jcore = f32[5,128,128]{2,1,0:T(8,128)S(1)} collective-permute-done((f32[5,128,128]{2,1,0:T(8,128)}, f32[5,128,128]{2,1,0:T(8,128)S(1)}, u32[]{:S(2)}, u32[]{:S(2)}) %collective-permute-start.8) | collective-permute-done | bytes 327712 | tf_op jit(solution)/shard_map/ppermute | solution.py:328
  9.7 2.1 %collective-permute-start.9 = (f32[5,128,128]{2,1,0:T(8,128)S(1)}, f32[5,128,128]{2,1,0:T(8,128)S(1)}, u32[]{:S(2)}, u32[]{:S(2)}) collective-permute-start(f32[5,128,128]{2,1,0:T(8,128)S(1)} %collective-permute-done.8.jcore), channel_id=1, source_target_pairs={{0,1},{1,0},{2,3},{3,2},{4,5},{5,4},{6,7},{7,6},{8,9},{9,8},{10,11... | collective-permute-start | bytes 983048 | tf_op jit(solution)/shard_map/ppermute | solution.py:321
  11.8 0.0 collective-permute-done.5.jcore
  11.8 7.6 %collective-permute-start.6 = (f32[5,128,128]{2,1,0:T(8,128)S(1)}, f32[5,128,128]{2,1,0:T(8,128)S(1)}, u32[]{:S(2)}, u32[]{:S(2)}) collective-permute-start(f32[5,128,128]{2,1,0:T(8,128)S(1)} %collective-permute-done.5.jcore), channel_id=1, source_target_pairs={{0,1},{1,0},{2,3},{3,2},{4,5},{5,4},{6,7},{7,6},{8,9},{9,8},{10,11... | collective-permute-start | bytes 983048 | tf_op jit(solution)/shard_map/ppermute | solution.py:321
  19.4 0.0 collective-permute-done.jcore
  19.4 0.1 collective-permute-start.1
  19.5 0.0 collective-permute-done.3.near
  19.5 1.3 %collective-permute-start.4 = (f32[5,128,128]{2,1,0:T(8,128)S(1)}, f32[5,128,128]{2,1,0:T(8,128)S(1)}, u32[]{:S(2)}, u32[]{:S(2)}) collective-permute-start(f32[5,128,128]{2,1,0:T(8,128)S(1)} %collective-permute-done.3.near), channel_id=1, source_target_pairs={{0,2},{2,4},{4,6},{3,1},{5,3},{7,5},{8,10},{10,12},{12,14},{11,9},... | collective-permute-start | bytes 983048 | tf_op jit(solution)/shard_map/ppermute | solution.py:322
  20.8 0.0 collective-permute-done.9.jnear
  20.8 1.3 %collective-permute-start.10 = (f32[5,128,128]{2,1,0:T(8,128)S(1)}, f32[5,128,128]{2,1,0:T(8,128)}, u32[]{:S(2)}, u32[]{:S(2)}) collective-permute-start(f32[5,128,128]{2,1,0:T(8,128)S(1)} %collective-permute-done.9.jnear), channel_id=1, source_target_pairs={{0,2},{2,4},{4,6},{3,1},{5,3},{7,5},{8,10},{10,12},{12,14},{11,9},... | collective-permute-start | bytes 983048 | tf_op jit(solution)/shard_map/ppermute | solution.py:322
  22.1 0.0 collective-permute-done.6.jnear
  22.1 1.3 %collective-permute-start.7 = (f32[5,128,128]{2,1,0:T(8,128)S(1)}, f32[5,128,128]{2,1,0:T(8,128)S(1)}, u32[]{:S(2)}, u32[]{:S(2)}) collective-permute-start(f32[5,128,128]{2,1,0:T(8,128)S(1)} %collective-permute-done.6.jnear), channel_id=1, source_target_pairs={{0,2},{2,4},{4,6},{3,1},{5,3},{7,5},{8,10},{10,12},{12,14},{11,9},... | collective-permute-start | bytes 983048 | tf_op jit(solution)/shard_map/ppermute | solution.py:322
  23.4 0.0 collective-permute-done.1.jnear
  23.4 1.3 %collective-permute-start.2 = (f32[5,128,128]{2,1,0:T(8,128)S(1)}, f32[5,128,128]{2,1,0:T(8,128)S(1)}, u32[]{:S(2)}, u32[]{:S(2)}) collective-permute-start(f32[5,128,128]{2,1,0:T(8,128)S(1)} %collective-permute-done.1.jnear), channel_id=1, source_target_pairs={{0,2},{2,4},{4,6},{3,1},{5,3},{7,5},{8,10},{10,12},{12,14},{11,9},... | collective-permute-start | bytes 983048 | tf_op jit(solution)/shard_map/ppermute | solution.py:322
  24.7 2.6 %collective-permute-done.4.far = f32[5,128,128]{2,1,0:T(8,128)S(1)} collective-permute-done((f32[5,128,128]{2,1,0:T(8,128)S(1)}, f32[5,128,128]{2,1,0:T(8,128)S(1)}, u32[]{:S(2)}, u32[]{:S(2)}) %collective-permute-start.4) | collective-permute-done | bytes 327712 | tf_op jit(solution)/shard_map/ppermute | solution.py:322
  27.3 0.7 %copy-done.4 = f32[5,128,128]{2,1,0:T(8,128)} copy-done((f32[5,128,128]{2,1,0:T(8,128)}, f32[5,128,128]{2,1,0:T(8,128)S(1)}, u32[]{:S(2)}) %copy-start.4) | copy-done | bytes 327704
  28.0 4.9 %own.1 = (f32[13,128,128]{2,1,0:T(8,128)}, f32[5,128,128]{2,1,0:T(8,128)}, f32[5,128,128]{2,1,0:T(8,128)}, f32[5,128,128]{2,1,0:T(8,128)}, f32[33,128,128]{2,1,0:T(8,128)}) custom-call(f32[5,128,128]{2,1,0:T(8,128)} %bitcast.5, f32[5,128,128]{2,1,0:T(8,128)} %copy-done.3, f32[5,128,128]{2,1,0:T(8,128)} %copy-done.4, s32[4]{0:T(128)} %index_ref.5, ...), custom_call_target="tpu_custom_call" | custom-call | flops 20000000 | bytes 4980768 | tf_op jit(solution)/shard_map/own/pallas_call | solution.py:299
  32.9 0.0 collective-permute-done.10.jfar
  32.9 4.6 %pair.3.acc_ref = f32[5,128,128]{2,1,0:T(8,128)} custom-call(f32[5,128,128]{2,1,0:T(8,128)} %copy-done.6, f32[5,128,128]{2,1,0:T(8,128)} %copy-done.8, f32[5,128,128]{2,1,0:T(8,128)} %collective-permute-done.10.jfar, f32[13,128,128]{2,1,0:T(8,128)} %get-tuple-element.13.window, f32[5,128,128]{2,1,0:T(8,128)} %get-tuple-element.14.mean_ref, ...), custom_call_target="tpu_custom_call" | custom-call | flops 20000000 | bytes 3145760 | tf_op jit(solution)/shard_map/pair/pallas_call | solution.py:299
  37.5 0.7 %copy-done.9 = f32[5,128,128]{2,1,0:T(8,128)} copy-done((f32[5,128,128]{2,1,0:T(8,128)}, f32[5,128,128]{2,1,0:T(8,128)S(1)}, u32[]{:S(2)}) %copy-start.9) | copy-done | bytes 327704
  38.3 4.6 %pair.4.acc_ref = f32[5,128,128]{2,1,0:T(8,128)} custom-call(f32[5,128,128]{2,1,0:T(8,128)} %copy-done.5, f32[5,128,128]{2,1,0:T(8,128)} %copy-done.7, f32[5,128,128]{2,1,0:T(8,128)} %copy-done.9, f32[13,128,128]{2,1,0:T(8,128)} %get-tuple-element.13.window, f32[5,128,128]{2,1,0:T(8,128)} %get-tuple-element.14.mean_ref, ...), custom_call_target="tpu_custom_call" | custom-call | flops 20000000 | bytes 3145760 | tf_op jit(solution)/shard_map/pair/pallas_call | solution.py:299
  42.9 0.7 %copy-done.2 = f32[5,128,128]{2,1,0:T(8,128)} copy-done((f32[5,128,128]{2,1,0:T(8,128)}, f32[5,128,128]{2,1,0:T(8,128)S(1)}, u32[]{:S(2)}) %copy-start.2) | copy-done | bytes 327704
  43.6 4.8 %pair.5 = (f32[5,128,128]{2,1,0:T(8,128)}, f32[3,128,128]{2,1,0:T(8,128)}, f32[3,128,128]{2,1,0:T(8,128)}) custom-call(f32[5,128,128]{2,1,0:T(8,128)} %copy-done, f32[5,128,128]{2,1,0:T(8,128)} %copy-done.1, f32[5,128,128]{2,1,0:T(8,128)} %copy-done.2, f32[13,128,128]{2,1,0:T(8,128)} %get-tuple-element.13.window, f32[5,128,128]{2,1,0:T(8,128)} %get-tuple-element.14.mean_ref, ...), custom_call_target="tpu_custom_call" | custom-call | flops 20000000 | bytes 3538976 | tf_op jit(solution)/shard_map/pair/pallas_call | solution.py:299
  48.4 5.1 %collective-permute-start.11 = (f32[3,128,128]{2,1,0:T(8,128)}, f32[3,128,128]{2,1,0:T(8,128)S(1)}, u32[]{:S(2)}, u32[]{:S(2)}) collective-permute-start(f32[3,128,128]{2,1,0:T(8,128)} %get-tuple-element.18), channel_id=1, source_target_pairs={{0,1},{1,0},{2,3},{3,2},{4,5},{5,4},{6,7},{7,6},{8,9},{9,8},{10,11... | collective-permute-start | bytes 589832 | tf_op jit(solution)/shard_map/ppermute | solution.py:364
  53.5 1.9 %collective-permute-start.12 = (f32[3,128,128]{2,1,0:T(8,128)}, f32[3,128,128]{2,1,0:T(8,128)S(1)}, u32[]{:S(2)}, u32[]{:S(2)}) collective-permute-start(f32[3,128,128]{2,1,0:T(8,128)} %get-tuple-element.19), channel_id=1, source_target_pairs={{1,2},{3,4},{5,6},{2,1},{4,3},{6,5},{9,10},{11,12},{13,14},{10,9},... | collective-permute-start | bytes 589832 | tf_op jit(solution)/shard_map/ppermute | solution.py:365
  55.5 5.3 %collective-permute-done.12.cfar = f32[3,128,128]{2,1,0:T(8,128)S(1)} collective-permute-done((f32[3,128,128]{2,1,0:T(8,128)}, f32[3,128,128]{2,1,0:T(8,128)S(1)}, u32[]{:S(2)}, u32[]{:S(2)}) %collective-permute-start.12) | collective-permute-done | bytes 196640 | tf_op jit(solution)/shard_map/ppermute | solution.py:365
  60.7 0.7 copy-done.11
  61.4 5.6 %smooth.1 = f32[3,1,5,128,128]{4,3,2,1,0:T(8,128)} custom-call(f32[5,128,128]{2,1,0:T(8,128)} %get-tuple-element.17.coeff, f32[3,128,128]{2,1,0:T(8,128)} %copy-done.10, f32[3,128,128]{2,1,0:T(8,128)} %copy-done.11, f32[33,128,128]{2,1,0:T(8,128)} %get-tuple-element.20.grads, f32[3,1,5,128,128]{4,3,2,1,0:T(8,128)} %velocity.1), custom_call_target="tpu_custom_call" | custom-call | flops 20000000 | bytes 6000000 | tf_op jit(solution)/shard_map/smooth/pallas_call | solution.py:368
  (23 shorter events, 0.0 us)
Async XLA Ops:
  0.0 9.7 %collective-permute-start.8 = (f32[5,128,128]{2,1,0:T(8,128)}, f32[5,128,128]{2,1,0:T(8,128)S(1)}, u32[]{:S(2)}, u32[]{:S(2)}) collective-permute-start(f32[5,128,128]{2,1,0:T(8,128)} %bitcast.1), channel_id=1, source_target_pairs={{0,8},{8,0},{16,24},{24,16},{1,9},{9,1},{17,25},{25,17},{2,10},{10... | collective-permute-start | bytes 983048 | tf_op jit(solution)/shard_map/ppermute | solution.py:328
  2.0 9.7 %collective-permute-start.5 = (f32[5,128,128]{2,1,0:T(8,128)}, f32[5,128,128]{2,1,0:T(8,128)S(1)}, u32[]{:S(2)}, u32[]{:S(2)}) collective-permute-start(f32[5,128,128]{2,1,0:T(8,128)} %bitcast.2), channel_id=1, source_target_pairs={{0,16},{8,24},{16,0},{24,8},{1,17},{9,25},{17,1},{25,9},{2,18},{10... | collective-permute-start | bytes 983048 | tf_op jit(solution)/shard_map/ppermute | solution.py:328
  3.3 16.1 %collective-permute-start = (f32[5,128,128]{2,1,0:T(8,128)}, f32[5,128,128]{2,1,0:T(8,128)S(1)}, u32[]{:S(2)}, u32[]{:S(2)}) collective-permute-start(f32[5,128,128]{2,1,0:T(8,128)} %bitcast.3), channel_id=1, source_target_pairs={{0,24},{8,16},{16,8},{24,0},{1,25},{9,17},{17,9},{25,1},{2,26},{10... | collective-permute-start | bytes 983048 | tf_op jit(solution)/shard_map/ppermute | solution.py:328
  3.3 16.2 %collective-permute-start.3 = (f32[5,128,128]{2,1,0:T(8,128)}, f32[5,128,128]{2,1,0:T(8,128)S(1)}, u32[]{:S(2)}, u32[]{:S(2)}) collective-permute-start(f32[5,128,128]{2,1,0:T(8,128)} %bitcast.4), channel_id=1, source_target_pairs={{0,1},{1,0},{2,3},{3,2},{4,5},{5,4},{6,7},{7,6},{8,9},{9,8},{10,11... | collective-permute-start | bytes 983048 | tf_op jit(solution)/shard_map/ppermute | solution.py:321
  9.7 23.2 %copy-start.6 = (f32[5,128,128]{2,1,0:T(8,128)}, f32[5,128,128]{2,1,0:T(8,128)S(1)}, u32[]{:S(2)}) copy-start(f32[5,128,128]{2,1,0:T(8,128)S(1)} %collective-permute-done.8.jcore) | copy-start | bytes 983044
  9.7 11.1 %collective-permute-start.9 = (f32[5,128,128]{2,1,0:T(8,128)S(1)}, f32[5,128,128]{2,1,0:T(8,128)S(1)}, u32[]{:S(2)}, u32[]{:S(2)}) collective-permute-start(f32[5,128,128]{2,1,0:T(8,128)S(1)} %collective-permute-done.8.jcore), channel_id=1, source_target_pairs={{0,1},{1,0},{2,3},{3,2},{4,5},{5,4},{6,7},{7,6},{8,9},{9,8},{10,11... | collective-permute-start | bytes 983048 | tf_op jit(solution)/shard_map/ppermute | solution.py:321
  11.8 25.8 %copy-start.5 = (f32[5,128,128]{2,1,0:T(8,128)}, f32[5,128,128]{2,1,0:T(8,128)S(1)}, u32[]{:S(2)}) copy-start(f32[5,128,128]{2,1,0:T(8,128)S(1)} %collective-permute-done.5.jcore) | copy-start | bytes 983044
  11.8 10.3 %collective-permute-start.6 = (f32[5,128,128]{2,1,0:T(8,128)S(1)}, f32[5,128,128]{2,1,0:T(8,128)S(1)}, u32[]{:S(2)}, u32[]{:S(2)}) collective-permute-start(f32[5,128,128]{2,1,0:T(8,128)S(1)} %collective-permute-done.5.jcore), channel_id=1, source_target_pairs={{0,1},{1,0},{2,3},{3,2},{4,5},{5,4},{6,7},{7,6},{8,9},{9,8},{10,11... | collective-permute-start | bytes 983048 | tf_op jit(solution)/shard_map/ppermute | solution.py:321
  19.4 23.5 %copy-start = (f32[5,128,128]{2,1,0:T(8,128)}, f32[5,128,128]{2,1,0:T(8,128)S(1)}, u32[]{:S(2)}) copy-start(f32[5,128,128]{2,1,0:T(8,128)S(1)} %collective-permute-done.jcore) | copy-start | bytes 983044
  19.4 4.0 %collective-permute-start.1 = (f32[5,128,128]{2,1,0:T(8,128)S(1)}, f32[5,128,128]{2,1,0:T(8,128)S(1)}, u32[]{:S(2)}, u32[]{:S(2)}) collective-permute-start(f32[5,128,128]{2,1,0:T(8,128)S(1)} %collective-permute-done.jcore), channel_id=1, source_target_pairs={{0,1},{1,0},{2,3},{3,2},{4,5},{5,4},{6,7},{7,6},{8,9},{9,8},{10,11... | collective-permute-start | bytes 983048 | tf_op jit(solution)/shard_map/ppermute | solution.py:321
  19.5 7.8 %copy-start.3 = (f32[5,128,128]{2,1,0:T(8,128)}, f32[5,128,128]{2,1,0:T(8,128)S(1)}, u32[]{:S(2)}) copy-start(f32[5,128,128]{2,1,0:T(8,128)S(1)} %collective-permute-done.3.near) | copy-start | bytes 983044
  19.5 7.8 %collective-permute-start.4 = (f32[5,128,128]{2,1,0:T(8,128)S(1)}, f32[5,128,128]{2,1,0:T(8,128)S(1)}, u32[]{:S(2)}, u32[]{:S(2)}) collective-permute-start(f32[5,128,128]{2,1,0:T(8,128)S(1)} %collective-permute-done.3.near), channel_id=1, source_target_pairs={{0,2},{2,4},{4,6},{3,1},{5,3},{7,5},{8,10},{10,12},{12,14},{11,9},... | collective-permute-start | bytes 983048 | tf_op jit(solution)/shard_map/ppermute | solution.py:322
  20.8 12.1 %copy-start.8 = (f32[5,128,128]{2,1,0:T(8,128)}, f32[5,128,128]{2,1,0:T(8,128)S(1)}, u32[]{:S(2)}) copy-start(f32[5,128,128]{2,1,0:T(8,128)S(1)} %collective-permute-done.9.jnear) | copy-start | bytes 983044
  20.8 12.1 %collective-permute-start.10 = (f32[5,128,128]{2,1,0:T(8,128)S(1)}, f32[5,128,128]{2,1,0:T(8,128)}, u32[]{:S(2)}, u32[]{:S(2)}) collective-permute-start(f32[5,128,128]{2,1,0:T(8,128)S(1)} %collective-permute-done.9.jnear), channel_id=1, source_target_pairs={{0,2},{2,4},{4,6},{3,1},{5,3},{7,5},{8,10},{10,12},{12,14},{11,9},... | collective-permute-start | bytes 983048 | tf_op jit(solution)/shard_map/ppermute | solution.py:322
  22.1 15.4 %copy-start.7 = (f32[5,128,128]{2,1,0:T(8,128)}, f32[5,128,128]{2,1,0:T(8,128)S(1)}, u32[]{:S(2)}) copy-start(f32[5,128,128]{2,1,0:T(8,128)S(1)} %collective-permute-done.6.jnear) | copy-start | bytes 983044
  22.1 15.4 %collective-permute-start.7 = (f32[5,128,128]{2,1,0:T(8,128)S(1)}, f32[5,128,128]{2,1,0:T(8,128)S(1)}, u32[]{:S(2)}, u32[]{:S(2)}) collective-permute-start(f32[5,128,128]{2,1,0:T(8,128)S(1)} %collective-permute-done.6.jnear), channel_id=1, source_target_pairs={{0,2},{2,4},{4,6},{3,1},{5,3},{7,5},{8,10},{10,12},{12,14},{11,9},... | collective-permute-start | bytes 983048 | tf_op jit(solution)/shard_map/ppermute | solution.py:322
  23.4 19.5 %copy-start.1 = (f32[5,128,128]{2,1,0:T(8,128)}, f32[5,128,128]{2,1,0:T(8,128)S(1)}, u32[]{:S(2)}) copy-start(f32[5,128,128]{2,1,0:T(8,128)S(1)} %collective-permute-done.1.jnear) | copy-start | bytes 983044
  23.4 19.5 %collective-permute-start.2 = (f32[5,128,128]{2,1,0:T(8,128)S(1)}, f32[5,128,128]{2,1,0:T(8,128)S(1)}, u32[]{:S(2)}, u32[]{:S(2)}) collective-permute-start(f32[5,128,128]{2,1,0:T(8,128)S(1)} %collective-permute-done.1.jnear), channel_id=1, source_target_pairs={{0,2},{2,4},{4,6},{3,1},{5,3},{7,5},{8,10},{10,12},{12,14},{11,9},... | collective-permute-start | bytes 983048 | tf_op jit(solution)/shard_map/ppermute | solution.py:322
  27.3 0.7 %copy-start.4 = (f32[5,128,128]{2,1,0:T(8,128)}, f32[5,128,128]{2,1,0:T(8,128)S(1)}, u32[]{:S(2)}) copy-start(f32[5,128,128]{2,1,0:T(8,128)S(1)} %collective-permute-done.4.far) | copy-start | bytes 983044
  37.5 0.8 %copy-start.9 = (f32[5,128,128]{2,1,0:T(8,128)}, f32[5,128,128]{2,1,0:T(8,128)S(1)}, u32[]{:S(2)}) copy-start(f32[5,128,128]{2,1,0:T(8,128)S(1)} %collective-permute-done.7.jfar) | copy-start | bytes 983044
  42.9 0.7 %copy-start.2 = (f32[5,128,128]{2,1,0:T(8,128)}, f32[5,128,128]{2,1,0:T(8,128)S(1)}, u32[]{:S(2)}) copy-start(f32[5,128,128]{2,1,0:T(8,128)S(1)} %collective-permute-done.2.jfar) | copy-start | bytes 983044
  48.4 7.0 %collective-permute-start.11 = (f32[3,128,128]{2,1,0:T(8,128)}, f32[3,128,128]{2,1,0:T(8,128)S(1)}, u32[]{:S(2)}, u32[]{:S(2)}) collective-permute-start(f32[3,128,128]{2,1,0:T(8,128)} %get-tuple-element.18), channel_id=1, source_target_pairs={{0,1},{1,0},{2,3},{3,2},{4,5},{5,4},{6,7},{7,6},{8,9},{9,8},{10,11... | collective-permute-start | bytes 589832 | tf_op jit(solution)/shard_map/ppermute | solution.py:364
  53.5 7.2 %collective-permute-start.12 = (f32[3,128,128]{2,1,0:T(8,128)}, f32[3,128,128]{2,1,0:T(8,128)S(1)}, u32[]{:S(2)}, u32[]{:S(2)}) collective-permute-start(f32[3,128,128]{2,1,0:T(8,128)} %get-tuple-element.19), channel_id=1, source_target_pairs={{1,2},{3,4},{5,6},{2,1},{4,3},{6,5},{9,10},{11,12},{13,14},{10,9},... | collective-permute-start | bytes 589832 | tf_op jit(solution)/shard_map/ppermute | solution.py:365
  55.5 5.3 %copy-start.10 = (f32[3,128,128]{2,1,0:T(8,128)}, f32[3,128,128]{2,1,0:T(8,128)S(1)}, u32[]{:S(2)}) copy-start(f32[3,128,128]{2,1,0:T(8,128)S(1)} %collective-permute-done.11.cnear) | copy-start | bytes 589828
  60.7 0.7 %copy-start.11 = (f32[3,128,128]{2,1,0:T(8,128)}, f32[3,128,128]{2,1,0:T(8,128)S(1)}, u32[]{:S(2)}) copy-start(f32[3,128,128]{2,1,0:T(8,128)S(1)} %collective-permute-done.12.cfar) | copy-start | bytes 589828
